TPU v7x, 512 devices: a whole 4x4x16 slice. The times are simulated.
512 devices in a mesh: dp: 32 (over x, y, core), expert: 16 (over z).
Axes of the slice: x: 4, y: 4, z: 16, core: 2. Of those that a mesh axis runs over, the one named last changes fastest.
Arguments:
- tokens: bfloat16 [65536, 7168], P(('dp', 'expert')), may hold values from -6 to 6
- route_ids: int32 [65536, 8], P(('dp', 'expert')), may hold values from 0 to 255, as said below
- route_gates: float32 [65536, 8], P(('dp', 'expert')), may hold values from 0.1 to 1
- gate_up: bfloat16 [2, 7168, 2048], P(None, 'dp', 'expert'), may hold values from -0.0625 to 0.0625
- down_weight: bfloat16 [2048, 7168], P('expert', 'dp'), may hold values from -0.125 to 0.125
Outputs:
- mixed: bfloat16 [65536, 7168], P(('dp', 'expert'))
Inputs may be any that keep to these rules, and one draw needn't show every extreme that they name: `route_ids`: each token names 8 different experts. Among the 128 rows of one device, each expert below 1 is named by 1 to 12 rows; for each such expert, in every draw some run of 16 consecutive devices' blocks (aligned at multiples of 16) has exactly 12 rows naming it in every block.
All inputs are finite; a program needn't handle non-finite values.
Results may differ from a plain program's by a relative error of at most 0.0057.
Values may be sent and summed in bfloat16 or wider, within the bound.
No kernel may reach another device: no remote copies, remote signals or barrier semaphores. Data moves between devices by JAX's collectives and lax.ppermute only.
A program may use at most 64 MiB of HBM per device.

v0:
```python
import jax
import jax.numpy as jnp
from jax import lax
from jax.sharding import PartitionSpec as P

EXPERTS = 1
CAP = 12


def body(tokens, route_ids, route_gates, gate_up, down_weight):
    model_width = tokens.shape[1]
    matches = route_ids == 0
    routed = jnp.any(matches, axis=1)
    weight = jnp.sum(jnp.where(matches, route_gates, 0.0), axis=1)
    places = jnp.cumsum(routed.astype(jnp.int32)) - 1
    capacity_ids = jnp.arange(CAP, dtype=jnp.int32)
    packing = (routed[None, :] & (places[None, :] == capacity_ids[:, None])).astype(jnp.bfloat16)
    packed = jnp.dot(packing, tokens, preferred_element_type=jnp.float32).astype(jnp.bfloat16)
    dispatched = lax.all_gather(packed, "expert", axis=0, tiled=True)
    gu = lax.all_gather(gate_up, "dp", axis=1, tiled=True)
    dn = lax.all_gather(down_weight, "dp", axis=1, tiled=True)
    projected = jnp.einsum("rd,gdf->grf", dispatched, gu, preferred_element_type=jnp.float32)
    hidden = (jax.nn.silu(projected[0]) * projected[1]).astype(jnp.bfloat16)
    partial_value = jnp.dot(hidden, dn, preferred_element_type=jnp.float32).astype(jnp.bfloat16)
    summed = lax.psum_scatter(partial_value, "expert", scatter_dimension=0, tiled=True)
    selector = routed[:, None] & (places[:, None] == capacity_ids[None, :])
    scaled = jnp.where(selector, weight[:, None], 0.0)
    mixed = jnp.dot(
        scaled,
        summed.astype(jnp.float32),
        precision=lax.Precision.HIGHEST,
        preferred_element_type=jnp.float32,
    )
    return mixed.astype(jnp.bfloat16)


def solution(mesh):
    return jax.shard_map(
        body,
        mesh=mesh,
        in_specs=(
            P(("dp", "expert"), None),
            P(("dp", "expert"), None),
            P(("dp", "expert"), None),
            P(None, "dp", "expert"),
            P("expert", "dp"),
        ),
        out_specs=P(("dp", "expert"), None),
        check_vma=False,
    )
```

profile of v0, /device:TPU:96, one launch (start us, length us, event | category | flops | bytes accessed | tf_op | source)
XLA Modules:
  0.0 334.5 jit_solution(3972932187216507593)
XLA Ops:
  6.5 0.0 copy-start
  6.5 0.0 all-gather.9.cloned.1.call-start
  6.5 0.9 select_reduce_fusion
  7.4 0.1 copy.8
  7.5 0.2 reduce-window.7
  7.7 0.1 add_reduce_fusion
  7.8 0.3 copy-done
  8.1 1.0 fusion.1
  9.1 0.0 all-gather.9.cloned.1.call-update
  9.1 0.0 all-gather.5.cloned.1.call-start
  9.2 0.7 all-gather.5.cloned.1.call-update
  9.9 0.0 all-gather.7.cloned.1.call-start
  9.9 0.7 all-gather.7.cloned.1.call-update
  10.6 78.2 %all-gather.9.cloned.1.call-done = bf16[16,12,7168]{2,1,0:T(8,128)(2,1)} async-done(((bf16[1,12,7168]{2,1,0:T(8,128)(2,1)}), bf16[16,12,7168]{2,1,0:T(8,128)(2,1)}) %all-gather.9.cloned.1.call-update) | async-done | bytes 2752528 | tf_op jit(solution)/shard_map/all_gather | solution.py:19
  88.8 4.5 %reshape.35 = bf16[192,7168,1]{1,0,2:T(8,128)(2,1)} reshape(bf16[16,12,7168]{2,1,0:T(8,128)(2,1)} %all-gather.9.cloned.1.call-done) | data formatting | bytes 5505024
  93.3 57.5 %all-gather.5.cloned.1.call-done = bf16[2,7168,128]{2,1,0:T(8,128)(2,1)} async-done(((bf16[2,224,128]{2,1,0:T(8,128)(2,1)}), bf16[2,7168,128]{2,1,0:T(8,128)(2,1)}) %all-gather.5.cloned.1.call-update) | async-done | bytes 3670032 | tf_op jit(solution)/shard_map/all_gather | solution.py:20
  150.7 3.8 %convolution_bitcast_fusion = f32[2,192,128]{2,1,0:T(8,128)S(1)} fusion(bf16[192,7168,1]{1,0,2:T(8,128)(2,1)} %reshape.35, bf16[2,7168,128]{2,1,0:T(8,128)(2,1)} %all-gather.5.cloned.1.call-done), kind=kOutput, calls=%fused_computation.4 | convolution fusion | flops 704643072 | bytes 6619136 | tf_op jit(solution)/shard_map/rd,gdf->grf/dot_general | solution.py:22
  154.5 57.5 %all-gather.7.cloned.1.call-done = bf16[128,7168]{0,1:T(8,128)(2,1)} async-done(((bf16[128,224]{0,1:T(8,128)(2,1)}), bf16[128,7168]{0,1:T(8,128)(2,1)}) %all-gather.7.cloned.1.call-update) | async-done | bytes 1835024 | tf_op jit(solution)/shard_map/all_gather | solution.py:21
  212.0 3.9 %convolution_convert_fusion = bf16[192,7168]{1,0:T(8,128)(2,1)} fusion(bf16[128,7168]{0,1:T(8,128)(2,1)} %all-gather.7.cloned.1.call-done, f32[2,192,128]{2,1,0:T(8,128)S(1)} %convolution_bitcast_fusion), kind=kOutput, calls=%fused_computation | convolution fusion | flops 353845248 | bytes 4784128 | tf_op jit(solution)/shard_map/dot_general | solution.py:24
  215.9 46.2 %fusion = bf16[16,7168]{1,0:T(8,128)(2,1)S(1)} fusion(bf16[192,7168]{1,0:T(8,128)(2,1)} %convolution_convert_fusion), kind=kCustom, calls=%all-reduce-scatter | all-reduce-scatter fusion | flops 1835009 | bytes 2983936
  262.1 5.4 %collective-permute-start = (bf16[16,7168]{1,0:T(8,128)(2,1)S(1)}, bf16[16,7168]{1,0:T(8,128)(2,1)S(1)}, u32[]{:S(2)}, u32[]{:S(2)}) collective-permute-start(bf16[16,7168]{1,0:T(8,128)(2,1)S(1)} %fusion), channel_id=1, source_target_pairs={{0,1},{1,2},{2,3},{3,4},{4,5},{5,6},{6,7},{7,8},{8,9},{9,10},{10,1... | collective-permute-start | bytes 688136
  267.6 2.4 collective-permute-start.1
  270.0 6.7 %collective-permute-start.2 = (bf16[16,7168]{1,0:T(8,128)(2,1)S(1)}, bf16[16,7168]{1,0:T(8,128)(2,1)}, u32[]{:S(2)}, u32[]{:S(2)}) collective-permute-start(bf16[16,7168]{1,0:T(8,128)(2,1)S(1)} %fusion), channel_id=1, source_target_pairs={{0,3},{1,4},{2,5},{3,6},{4,7},{5,8},{6,9},{7,10},{8,11},{9,12},{10... | collective-permute-start | bytes 688136
  276.7 0.1 slice.10
  276.7 4.6 %collective-permute-start.3 = (bf16[12,7168]{1,0:T(8,128)(2,1)S(1)}, bf16[12,7168]{1,0:T(8,128)(2,1)S(1)}, u32[]{:S(2)}, u32[]{:S(2)}) collective-permute-start(bf16[12,7168]{1,0:T(8,128)(2,1)S(1)} %slice.10), channel_id=1, source_target_pairs={{0,4},{1,5},{2,6},{3,7},{4,8},{5,9},{6,10},{7,11},{8,12},{9,13},{1... | collective-permute-start | bytes 516104
  281.3 1.3 dynamic-slice.4
  283.2 32.7 %collective-permute-done.3 = bf16[12,7168]{1,0:T(8,128)(2,1)S(1)} collective-permute-done((bf16[12,7168]{1,0:T(8,128)(2,1)S(1)}, bf16[12,7168]{1,0:T(8,128)(2,1)S(1)}, u32[]{:S(2)}, u32[]{:S(2)}) %collective-permute-start.3) | collective-permute-done | bytes 172064
  315.9 0.0 copy-start.2
  315.9 0.0 collective-permute-done
  315.9 0.0 collective-permute-done.1
  315.9 0.7 copy-done.2
  316.6 0.0 copy-start.1
  316.6 0.7 copy-done.1
  317.3 0.0 collective-permute-done.2
  317.3 7.8 %concatenate = bf16[76,7168]{1,0:T(8,128)(2,1)S(1)} concatenate(bf16[12,7168]{1,0:T(8,128)(2,1)} %copy-done.2, bf16[16,7168]{1,0:T(8,128)(2,1)} %collective-permute-done.2, bf16[16,7168]{1,0:T(8,128)(2,1)} %copy-done.1, bf16[16,7168]{1,0:T(8,128)(2,1)S(1)} %collective-permute-done, bf16[16,7168]{1,0:T(8,128)(2,1)S(1)} %fusion), dimensions={0} | concatenate | bytes 2179072
  325.1 2.9 convolution_convert_fusion.1
  (2 shorter events, 0.0 us)
Async XLA Ops:
  6.5 1.5 copy-start
  6.5 82.2 %all-gather.9.cloned.1.call-start = ((), (), s32[]{:S(2)}) async-start(), calls=%async_computation.2 | async-start | bytes 3899392 | tf_op jit(solution)/shard_map/all_gather | solution.py:19
  9.1 141.6 %all-gather.5.cloned.1.call-start = ((), (), s32[]{:S(2)}) async-start(), calls=%async_computation | async-start | bytes 3784704 | tf_op jit(solution)/shard_map/all_gather | solution.py:20
  9.9 202.1 %all-gather.7.cloned.1.call-start = ((), (), s32[]{:S(2)}) async-start(), calls=%async_computation.1 | async-start | bytes 1892352 | tf_op jit(solution)/shard_map/all_gather | solution.py:21
  262.1 53.8 %collective-permute-start = (bf16[16,7168]{1,0:T(8,128)(2,1)S(1)}, bf16[16,7168]{1,0:T(8,128)(2,1)S(1)}, u32[]{:S(2)}, u32[]{:S(2)}) collective-permute-start(bf16[16,7168]{1,0:T(8,128)(2,1)S(1)} %fusion), channel_id=1, source_target_pairs={{0,1},{1,2},{2,3},{3,4},{4,5},{5,6},{6,7},{7,8},{8,9},{9,10},{10,1... | collective-permute-start | bytes 688136
  267.6 48.4 %collective-permute-start.1 = (bf16[16,7168]{1,0:T(8,128)(2,1)S(1)}, bf16[16,7168]{1,0:T(8,128)(2,1)S(1)}, u32[]{:S(2)}, u32[]{:S(2)}) collective-permute-start(bf16[16,7168]{1,0:T(8,128)(2,1)S(1)} %fusion), channel_id=1, source_target_pairs={{0,2},{1,3},{2,4},{3,5},{4,6},{5,7},{6,8},{7,9},{8,10},{9,11},{10,... | collective-permute-start | bytes 688136
  270.0 47.4 %collective-permute-start.2 = (bf16[16,7168]{1,0:T(8,128)(2,1)S(1)}, bf16[16,7168]{1,0:T(8,128)(2,1)}, u32[]{:S(2)}, u32[]{:S(2)}) collective-permute-start(bf16[16,7168]{1,0:T(8,128)(2,1)S(1)} %fusion), channel_id=1, source_target_pairs={{0,3},{1,4},{2,5},{3,6},{4,7},{5,8},{6,9},{7,10},{8,11},{9,12},{10... | collective-permute-start | bytes 688136
  276.7 39.2 %collective-permute-start.3 = (bf16[12,7168]{1,0:T(8,128)(2,1)S(1)}, bf16[12,7168]{1,0:T(8,128)(2,1)S(1)}, u32[]{:S(2)}, u32[]{:S(2)}) collective-permute-start(bf16[12,7168]{1,0:T(8,128)(2,1)S(1)} %slice.10), channel_id=1, source_target_pairs={{0,4},{1,5},{2,6},{3,7},{4,8},{5,9},{6,10},{7,11},{8,12},{9,13},{1... | collective-permute-start | bytes 516104
  315.9 0.7 copy-start.2
  316.6 0.7 copy-start.1
Sparse Core Ops, SparseCore 0:
  9.4 79.3 all-gather.8
  92.0 58.7 all-gather.4
  153.9 58.0 all-gather.6
where the time goes:
time: 335 us
  waiting for transfers between devices  227 us (68%)
  blocking collectives  46.2 us (14%)
  starting transfers between devices  19.2 us (6%)
  local copies, waits for them, and re-layouts  15.3 us (5%)
  between operations  13.8 us (4%)
  matrix products  11.6 us (3%)
    all_gather x1, waiting for transfers between devices, body(): dispatched = lax.all_gather(packed, 'expert', axis=0, tiled=True)  78.2 us
    all_gather x1, waiting for transfers between devices, body(): dn = lax.all_gather(down_weight, 'dp', axis=1, tiled=True)  57.5 us
    all_gather x1, waiting for transfers between devices, body(): gu = lax.all_gather(gate_up, 'dp', axis=1, tiled=True)  57.5 us
    unnamed x1, blocking collectives  46.2 us
    unnamed x7, waiting for transfers between devices  34.1 us
    unnamed x4, starting transfers between devices  19.1 us
    unnamed x10, local copies, waits for them, and re-layouts  15.2 us
  transfers between devices with their start and end apart: 7, of which 4 were waited for; matrix products, arithmetic and copies ran while one was open for 3% of the time, Pallas kernels for 0%

commit v1 on v0

--- a/solution.py
+++ b/solution.py
@@ -16,7 +16,9 @@
     capacity_ids = jnp.arange(CAP, dtype=jnp.int32)
     packing = (routed[None, :] & (places[None, :] == capacity_ids[:, None])).astype(jnp.bfloat16)
     packed = jnp.dot(packing, tokens, preferred_element_type=jnp.float32).astype(jnp.bfloat16)
-    dispatched = lax.all_gather(packed, "expert", axis=0, tiled=True)
+    dispatched = jnp.concatenate(
+        lax.all_to_all(jnp.stack([packed] * lax.axis_size("expert")), "expert", 0, 0), axis=0
+    )
     gu = lax.all_gather(gate_up, "dp", axis=1, tiled=True)
     dn = lax.all_gather(down_weight, "dp", axis=1, tiled=True)
     projected = jnp.einsum("rd,gdf->grf", dispatched, gu, preferred_element_type=jnp.float32)

time: 335 us -> 314 us (0.937)
  the two profiles are of different devices: /device:TPU:96 before, /device:TPU:120 now
where the time goes in v1:
time: 314 us; the launch traced here: 313 us
  waiting for transfers between devices  192 us (61%)
  blocking collectives  44.2 us (14%)
  starting transfers between devices  33.3 us (11%)
  local copies, waits for them, and re-layouts  17.6 us (6%)
  between operations  14.2 us (5%)
  matrix products  10.9 us (3%)
    all_to_all x1, waiting for transfers between devices, body(): lax.all_to_all(jnp.stack([packed] * lax.axis_size('expert')), 'expert', 0...  159 us
    unnamed x1, blocking collectives  44.2 us
    unnamed x6, waiting for transfers between devices  32.9 us
    unnamed x4, starting transfers between devices  18.9 us
    all_to_all x1, starting transfers between devices, body(): lax.all_to_all(jnp.stack([packed] * lax.axis_size('expert')), 'expert', 0...  14.3 us
    unnamed x9, local copies, waits for them, and re-layouts  10.7 us
  transfers between devices with their start and end apart: 7, of which 2 were waited for; matrix products, arithmetic and copies ran while one was open for 3% of the time, Pallas kernels for 0%

profile of v1, /device:TPU:120, one launch (start us, length us, event | category | flops | bytes accessed | tf_op | source)
XLA Modules:
  0.0 313.4 jit_solution(3588339475697003379)
XLA Ops:
  6.5 0.0 copy-start
  6.5 0.9 select_reduce_fusion
  7.4 0.1 copy.8
  7.5 0.2 reduce-window.7
  7.7 0.1 add_reduce_fusion
  7.8 0.3 copy-done
  8.1 0.3 convolution_convert_fusion.2
  8.4 2.3 stack.2
  10.7 14.3 %all-to-all-start = ((bf16[16,12,7168]{2,1,0:T(8,128)(2,1)}), bf16[16,12,7168]{2,1,0:T(8,128)(2,1)}, u32[]{:S(2)}, u32[]{:S(2)}) async-start(bf16[16,12,7168]{2,1,0:T(8,128)(2,1)} %stack.2), calls=%async_computation | async-start | bytes 7340032 | tf_op jit(solution)/shard_map/all_to_all | solution.py:20
  25.0 0.0 all-gather.3.cloned.1.call-start
  25.1 0.7 all-gather.3.cloned.1.call-update
  25.8 0.0 all-gather.5.cloned.1.call-start
  25.8 0.7 all-gather.5.cloned.1.call-update
  26.5 159.2 %all-to-all-done = bf16[16,12,7168]{2,1,0:T(8,128)(2,1)} async-done(((bf16[16,12,7168]{2,1,0:T(8,128)(2,1)}), bf16[16,12,7168]{2,1,0:T(8,128)(2,1)}, u32[]{:S(2)}, u32[]{:S(2)}) %all-to-all-start) | async-done | bytes 2752544 | tf_op jit(solution)/shard_map/all_to_all | solution.py:20
  185.7 4.5 %reshape.39 = bf16[192,7168,1]{1,0,2:T(8,128)(2,1)} reshape(bf16[16,12,7168]{2,1,0:T(8,128)(2,1)} %all-to-all-done) | data formatting | bytes 5505024 | tf_op jit(solution)/shard_map/reshape | solution.py:19
  190.2 0.0 all-gather.3.cloned.1.call-done
  190.2 3.8 %convolution_bitcast_fusion = f32[2,192,128]{2,1,0:T(8,128)S(1)} fusion(bf16[192,7168,1]{1,0,2:T(8,128)(2,1)} %reshape.39, bf16[2,7168,128]{2,1,0:T(8,128)(2,1)} %all-gather.3.cloned.1.call-done), kind=kOutput, calls=%fused_computation.3 | convolution fusion | flops 704643072 | bytes 6619136 | tf_op jit(solution)/shard_map/rd,gdf->grf/dot_general | solution.py:24
  193.9 0.0 all-gather.5.cloned.1.call-done
  193.9 3.9 %convolution_convert_fusion = bf16[192,7168]{1,0:T(8,128)(2,1)} fusion(bf16[128,7168]{0,1:T(8,128)(2,1)} %all-gather.5.cloned.1.call-done, f32[2,192,128]{2,1,0:T(8,128)S(1)} %convolution_bitcast_fusion), kind=kOutput, calls=%fused_computation | convolution fusion | flops 353845248 | bytes 4784128 | tf_op jit(solution)/shard_map/dot_general | solution.py:26
  197.9 44.2 %fusion = bf16[16,7168]{1,0:T(8,128)(2,1)S(1)} fusion(bf16[192,7168]{1,0:T(8,128)(2,1)} %convolution_convert_fusion), kind=kCustom, calls=%all-reduce-scatter | all-reduce-scatter fusion | flops 1835009 | bytes 2983936
  242.1 5.3 %collective-permute-start = (bf16[16,7168]{1,0:T(8,128)(2,1)S(1)}, bf16[16,7168]{1,0:T(8,128)(2,1)S(1)}, u32[]{:S(2)}, u32[]{:S(2)}) collective-permute-start(bf16[16,7168]{1,0:T(8,128)(2,1)S(1)} %fusion), channel_id=1, source_target_pairs={{0,1},{1,2},{2,3},{3,4},{4,5},{5,6},{6,7},{7,8},{8,9},{9,10},{10,1... | collective-permute-start | bytes 688136
  247.3 3.4 %collective-permute-start.1 = (bf16[16,7168]{1,0:T(8,128)(2,1)S(1)}, bf16[16,7168]{1,0:T(8,128)(2,1)S(1)}, u32[]{:S(2)}, u32[]{:S(2)}) collective-permute-start(bf16[16,7168]{1,0:T(8,128)(2,1)S(1)} %fusion), channel_id=1, source_target_pairs={{0,2},{1,3},{2,4},{3,5},{4,6},{5,7},{6,8},{7,9},{8,10},{9,11},{10,... | collective-permute-start | bytes 688136
  250.7 6.7 %collective-permute-start.2 = (bf16[16,7168]{1,0:T(8,128)(2,1)S(1)}, bf16[16,7168]{1,0:T(8,128)(2,1)}, u32[]{:S(2)}, u32[]{:S(2)}) collective-permute-start(bf16[16,7168]{1,0:T(8,128)(2,1)S(1)} %fusion), channel_id=1, source_target_pairs={{0,3},{1,4},{2,5},{3,6},{4,7},{5,8},{6,9},{7,10},{8,11},{9,12},{10... | collective-permute-start | bytes 688136
  257.4 0.1 slice.10
  257.5 3.6 %collective-permute-start.3 = (bf16[12,7168]{1,0:T(8,128)(2,1)S(1)}, bf16[12,7168]{1,0:T(8,128)(2,1)S(1)}, u32[]{:S(2)}, u32[]{:S(2)}) collective-permute-start(bf16[12,7168]{1,0:T(8,128)(2,1)S(1)} %slice.10), channel_id=1, source_target_pairs={{0,4},{1,5},{2,6},{3,7},{4,8},{5,9},{6,10},{7,11},{8,12},{9,13},{1... | collective-permute-start | bytes 516104
  261.1 1.3 dynamic-slice.4
  263.0 31.6 %collective-permute-done.3 = bf16[12,7168]{1,0:T(8,128)(2,1)S(1)} collective-permute-done((bf16[12,7168]{1,0:T(8,128)(2,1)S(1)}, bf16[12,7168]{1,0:T(8,128)(2,1)S(1)}, u32[]{:S(2)}, u32[]{:S(2)}) %collective-permute-start.3) | collective-permute-done | bytes 172064
  294.6 0.0 copy-start.2
  294.6 0.0 collective-permute-done
  294.6 0.0 collective-permute-done.1
  294.6 0.7 copy-done.2
  295.3 0.0 copy-start.1
  295.3 0.7 copy-done.1
  295.9 0.0 collective-permute-done.2
  295.9 7.8 %concatenate = bf16[76,7168]{1,0:T(8,128)(2,1)S(1)} concatenate(bf16[12,7168]{1,0:T(8,128)(2,1)} %copy-done.2, bf16[16,7168]{1,0:T(8,128)(2,1)} %collective-permute-done.2, bf16[16,7168]{1,0:T(8,128)(2,1)} %copy-done.1, bf16[16,7168]{1,0:T(8,128)(2,1)S(1)} %collective-permute-done, bf16[16,7168]{1,0:T(8,128)(2,1)S(1)} %fusion), dimensions={0} | concatenate | bytes 2179072
  303.7 2.9 convolution_convert_fusion.1
  (2 shorter events, 0.0 us)
Async XLA Ops:
  6.5 1.5 copy-start
  10.7 175.0 %all-to-all-start = ((bf16[16,12,7168]{2,1,0:T(8,128)(2,1)}), bf16[16,12,7168]{2,1,0:T(8,128)(2,1)}, u32[]{:S(2)}, u32[]{:S(2)}) async-start(bf16[16,12,7168]{2,1,0:T(8,128)(2,1)} %stack.2), calls=%async_computation | async-start | bytes 7340032 | tf_op jit(solution)/shard_map/all_to_all | solution.py:20
  25.0 165.1 %all-gather.3.cloned.1.call-start = ((), (), s32[]{:S(2)}) async-start(), calls=%async_computation.1 | async-start | bytes 3784704 | tf_op jit(solution)/shard_map/all_gather | solution.py:22
  25.8 168.2 %all-gather.5.cloned.1.call-start = ((), (), s32[]{:S(2)}) async-start(), calls=%async_computation.2 | async-start | bytes 1892352 | tf_op jit(solution)/shard_map/all_gather | solution.py:23
  242.1 52.5 %collective-permute-start = (bf16[16,7168]{1,0:T(8,128)(2,1)S(1)}, bf16[16,7168]{1,0:T(8,128)(2,1)S(1)}, u32[]{:S(2)}, u32[]{:S(2)}) collective-permute-start(bf16[16,7168]{1,0:T(8,128)(2,1)S(1)} %fusion), channel_id=1, source_target_pairs={{0,1},{1,2},{2,3},{3,4},{4,5},{5,6},{6,7},{7,8},{8,9},{9,10},{10,1... | collective-permute-start | bytes 688136
  247.3 47.2 %collective-permute-start.1 = (bf16[16,7168]{1,0:T(8,128)(2,1)S(1)}, bf16[16,7168]{1,0:T(8,128)(2,1)S(1)}, u32[]{:S(2)}, u32[]{:S(2)}) collective-permute-start(bf16[16,7168]{1,0:T(8,128)(2,1)S(1)} %fusion), channel_id=1, source_target_pairs={{0,2},{1,3},{2,4},{3,5},{4,6},{5,7},{6,8},{7,9},{8,10},{9,11},{10,... | collective-permute-start | bytes 688136
  250.7 45.2 %collective-permute-start.2 = (bf16[16,7168]{1,0:T(8,128)(2,1)S(1)}, bf16[16,7168]{1,0:T(8,128)(2,1)}, u32[]{:S(2)}, u32[]{:S(2)}) collective-permute-start(bf16[16,7168]{1,0:T(8,128)(2,1)S(1)} %fusion), channel_id=1, source_target_pairs={{0,3},{1,4},{2,5},{3,6},{4,7},{5,8},{6,9},{7,10},{8,11},{9,12},{10... | collective-permute-start | bytes 688136
  257.5 37.1 %collective-permute-start.3 = (bf16[12,7168]{1,0:T(8,128)(2,1)S(1)}, bf16[12,7168]{1,0:T(8,128)(2,1)S(1)}, u32[]{:S(2)}, u32[]{:S(2)}) collective-permute-start(bf16[12,7168]{1,0:T(8,128)(2,1)S(1)} %slice.10), channel_id=1, source_target_pairs={{0,4},{1,5},{2,6},{3,7},{4,8},{5,9},{6,10},{7,11},{8,12},{9,13},{1... | collective-permute-start | bytes 516104
  294.6 0.7 copy-start.2
  295.3 0.7 copy-start.1
Sparse Core Ops, SparseCore 0:
  29.0 61.3 all-gather.2
  93.5 57.9 all-gather.4
